TPU v7x, 32 devices: a whole 2x2x4 slice. The times are simulated.
32 devices in a mesh: parts: 2 (over y), sub: 4 (over z), row: 2 (over x), col: 2 (over core).
Axes of the slice: x: 2, y: 2, z: 4, core: 2. Of those that a mesh axis runs over, the one named last changes fastest.
Arguments:
- loads: float32 [8, 32, 1024], P(('parts', 'sub'), 'col'), parts along dimension 0, may hold values from -6 to 6
- weights: float32 [8, 1024], P(('parts', 'sub')), parts along dimension 0, may hold values from 0.25 to 4
- dual_ops: bfloat16 [8, 2048, 2048], P(('parts', 'sub'), 'row'), parts along dimension 0, as said below
- corner_maps: bfloat16 [8, 24, 2048], P(('parts', 'sub'), None, 'row'), parts along dimension 0, may hold values from -0.25 to 0.25
- coarse_inverse: float32 [96, 48], P('parts'), parts along dimension 0, as said below
- corner_ids: int32 [8, 24], P('parts'), parts along dimension 0, may hold values from 0 to 47, as said below
- iface_sizes: int32 [8], P('parts'), parts along dimension 0, may hold values from 512 to 1024, as said below
- left_partner: int32 [8, 1024], P(('parts', 'sub')), parts along dimension 0, may hold values from 0 to 1023, as said below
- right_partner: int32 [8, 1024], P(('parts', 'sub')), parts along dimension 0, may hold values from 0 to 1023, as said below
Outputs:
- solution: float32 [8, 32, 1024], P(('parts', 'sub'), 'col'), parts along dimension 0
- residual: float32 [8, 32, 1024], P(('parts', 'sub'), 'col'), parts along dimension 0
There are 2 independent parts, one for each index of `parts`. A program takes and returns all parts, laid end to end along the dimension named above; each array names one. Nothing has to cross between parts.
Inputs may be any that keep to these rules, and one draw needn't show every extreme that they name: Global indices 24/2 * s to 24/2 * s + 24/2 - 1 are the corners of the interface between s and s+1; the first half of subdomain s's corner_ids is a permutation of those of interface s-1, the second half a permutation of those of interface s. `left_partner`: each row s is a permutation that maps the slots below iface_sizes[s-1] onto slots below it. `right_partner`: each row s is a permutation that maps the slots below iface_sizes[s] onto slots below it, and is the inverse of left_partner[s+1]. `dual_ops`: symmetric positive definite. `coarse_inverse`: symmetric positive definite. For each s < 2, one of iface_sizes[s] and iface_sizes[s + 2] is 896 or more and the other 640 or less.
All inputs are finite; a program needn't handle non-finite values.
Results may differ from a plain program's by a relative error of at most 0.015.
Values may be sent and summed in bfloat16 or wider, within the bound.
No kernel may reach another device: no remote copies, remote signals or barrier semaphores. Data moves between devices by JAX's collectives and lax.ppermute only.
A program may use at most 64 MiB of HBM per device.

v0:
```python
import jax
import jax.numpy as jnp
from jax import lax
from jax.sharding import PartitionSpec as P

TILE = 128
ITERS = 2


def shifted(value, axis, steps):
    count = lax.axis_size(axis)
    pairs = [(source, (source + steps) % count) for source in range(count)]
    return lax.ppermute(value, axis, pairs)


def inner(first, second, half):
    return jnp.sum(first[:, :half] * second[:, :half], axis=1)


def paired_totals(residual, precond, image, half):
    return lax.psum((inner(residual, precond, half), inner(precond, image, half)), "sub")


def tile_products(vector, rows_op, first_tile, last_tile, output):

    def one_tile(tile_at, acc):
        piece = lax.dynamic_slice_in_dim(rows_op, tile_at * TILE, TILE, 0)
        product = lax.dot_general(
            vector, piece, (((1,), (1,)), ((), ())), preferred_element_type=jnp.float32
        )
        return lax.dynamic_update_slice_in_dim(acc, product, tile_at * TILE, 1)

    return lax.fori_loop(first_tile, last_tile, one_tile, output)


def live_tiles(size_before, size_after, block_start, block, half):
    left_live = jnp.clip(size_before - block_start, 0, block)
    right_live = jnp.clip(size_after - (block_start - half), 0, block)
    live_cols = jnp.where(block_start < half, left_live, right_live)
    return (live_cols + TILE - 1) // TILE


def per_device(
    loads,
    weights,
    dual_ops,
    corner_maps,
    coarse_inverse,
    corner_ids,
    iface_sizes,
    left_partner,
    right_partner,
):
    half = loads.shape[2]
    block = dual_ops.shape[1]
    width = coarse_inverse.shape[0]
    subdomain = lax.axis_index("sub")
    count = lax.axis_size("sub")
    row_index = lax.axis_index("row")
    left_map = left_partner[0]
    right_map = right_partner[0]
    slots = jnp.arange(half, dtype=jnp.int32)
    size_before = iface_sizes[(subdomain + count - 1) % count]
    size_after = iface_sizes[subdomain]
    live_left = (slots < size_before).astype(jnp.float32)
    live_right = (right_map < size_after).astype(jnp.float32)
    columns = jnp.arange(width, dtype=jnp.int32)
    own_hot = (corner_ids[subdomain][:, None] == columns[None, :]).astype(jnp.float32)
    operator = dual_ops[0]
    coupling = corner_maps[0]
    block_start = row_index * block
    own_tiles = live_tiles(size_before, size_after, block_start, block, half)

    def apply_operator(vec):
        halfway = vec.astype(jnp.bfloat16)
        empty = jnp.zeros((halfway.shape[0], block), jnp.float32)
        local = tile_products(halfway, operator, jnp.int32(0), own_tiles, empty)
        own_slots = lax.dynamic_slice_in_dim(halfway, row_index * block, block, 1)
        corner = lax.dot_general(
            own_slots, coupling, (((1,), (1,)), ((), ())), preferred_element_type=jnp.float32
        )
        scattered = jnp.dot(corner, own_hot, precision=lax.Precision.HIGHEST)
        coarse = lax.psum(scattered, ("sub", "row"))
        solved = jnp.dot(coarse, coarse_inverse, precision=lax.Precision.HIGHEST)
        back = lax.dot_general(
            solved, own_hot, (((1,), (1,)), ((), ())), precision=lax.Precision.HIGHEST
        ).astype(jnp.bfloat16)
        united = local + jnp.dot(back, coupling, preferred_element_type=jnp.float32)
        whole = lax.all_gather(united.astype(jnp.bfloat16), "row", axis=1, tiled=True).astype(
            united.dtype
        )
        lower = whole[:, :half]
        upper = whole[:, half:]
        arrived_left = shifted(upper.astype(jnp.bfloat16), "sub", 1).astype(upper.dtype)
        arrived_right = shifted(lower.astype(jnp.bfloat16), "sub", -1).astype(lower.dtype)
        result_left = (lower + jnp.take(arrived_left, left_map, axis=1)) * live_left
        result_right = (upper + jnp.take(arrived_right, right_map, axis=1)) * live_right
        return jnp.concatenate([result_left, result_right], axis=1)

    received = (
        shifted(loads[0].astype(jnp.bfloat16), "sub", -1).astype(jnp.float32),
        shifted(weights.astype(jnp.bfloat16), "sub", -1).astype(weights.dtype),
    )
    right_load = jnp.take(received[0], right_map, axis=1) * live_right
    right_weight = jnp.take(received[1], right_map, axis=1)
    residual = jnp.concatenate([loads[0] * live_left, right_load], axis=1)
    scaling = jnp.concatenate([weights, right_weight], axis=1)
    solution = jnp.zeros_like(residual)
    precond = scaling * residual
    image = apply_operator(precond)
    gamma, delta = paired_totals(residual, precond, image, half)
    alpha = gamma / delta
    direction = precond
    along = image
    for step in range(ITERS):
        solution = solution + alpha[:, None] * direction
        residual = residual - alpha[:, None] * along
        if step + 1 < ITERS:
            precond = scaling * residual
            image = apply_operator(precond)
            gamma_next, delta = paired_totals(residual, precond, image, half)
            ratio = gamma_next / gamma
            alpha = gamma_next / (delta - ratio * gamma_next / alpha)
            direction = precond + ratio[:, None] * direction
            along = image + ratio[:, None] * along
            gamma = gamma_next
    return (solution[:, :half][None], residual[:, :half][None])


def solution(mesh):
    placed = (
        P(("parts", "sub"), "col", None),
        P(("parts", "sub"), None),
        P(("parts", "sub"), "row", None),
        P(("parts", "sub"), None, "row"),
        P("parts", None),
        P("parts", None),
        P("parts"),
        P(("parts", "sub"), None),
        P(("parts", "sub"), None),
    )
    return jax.shard_map(
        per_device,
        mesh=mesh,
        in_specs=placed,
        out_specs=(P(("parts", "sub"), "col", None), P(("parts", "sub"), "col", None)),
        check_vma=False,
    )
```

profile of v0, /device:TPU:0, one launch (start us, length us, event | category | flops | bytes accessed | tf_op | source)
XLA Modules:
  0.0 136.2 jit_solution(17909804324471528583)
XLA Ops:
  1.5 5.1 %collective-permute-start.1 = (bf16[16,1024]{1,0:T(8,128)(2,1)S(1)}, bf16[16,1024]{1,0:T(8,128)(2,1)S(1)}, u32[]{:S(2)}, u32[]{:S(2)}) collective-permute-start(bf16[16,1024]{1,0:T(8,128)(2,1)S(1)} %bitcast_convert_fusion), channel_id=1, source_target_pairs={{0,12},{4,0},{8,4},{12,8},{1,13},{5,1},{9,5},{13,9},{2,14},{6,2},{... | collective-permute-start | bytes 98312 | tf_op jit(solution)/shard_map/ppermute | solution.py:13
  9.1 1.3 fusion.49
  10.5 1.3 fusion.35
  11.8 1.3 compare_convert_fusion
  16.7 4.5 %gather_fusion = f32[1024]{0:T(1024)S(1)} fusion(f32[1024]{0:T(1024)S(1)} %bitcast.80, s32[1024]{0:T(1024)S(1)} %broadcast_clamp_fusion), kind=kCustom, calls=%fused_computation.5 | custom fusion | bytes 12288 | tf_op jit(solution)/shard_map/jit(_take)/gather | solution.py:105
  21.5 2.8 %gather_fusion.1 = f32[1024,16]{1,0:T(8,128)S(1)} fusion(f32[16,1024]{0,1:T(8,128)S(1)} %copy.21, s32[1024]{0:T(1024)S(1)} %fusion.36), kind=kCustom, calls=%fused_computation.clone | custom fusion | bytes 135168 | tf_op jit(solution)/shard_map/jit(_take)/gather | solution.py:104
  24.5 10.4 %while.20 = (s32[]{:T(128)}, f32[16,1024]{1,0:T(8,128)S(1)}, s32[]{:T(128)}, bf16[1024,2048]{1,0:T(8,128)(2,1)}, bf16[16,2048]{1,0:T(8,128)(2,1)S(1)}, /*index=5*/s32[]{:T(128)}, s32[]{:T(128)}, s32[]{:T(128)}, s32[]{:T(128)}) while((s32[]{:T(128)}, f32[16,1024]{1,0:T(8,128)S(1)}, s32[]{:T(128)}, bf16[1024,2048]{1,0:T(8,128)(2,1)}, ...), condition=%wide.region_3.5_spmd, body=%wide.region_2.4_spmd.sunk | while | flops 8388614 | bytes 599179 | solution.py:33
  25.9 1.3 fusion.72
  27.1 1.3 fusion.72
  28.4 1.3 fusion.72
  31.0 1.3 fusion.72
  32.3 1.3 fusion.72
  33.6 1.3 fusion.72
  35.3 18.9 %psum.43 = f32[16,48]{1,0:T(8,128)S(1)} all-reduce(f32[16,48]{1,0:T(8,128)S(1)} %fusion.30), channel_id=1, replica_groups=mesh['parts'=2,'sub'=4,'row'=2,'col'=2] {'sub','row'}, use_global_device_ids=true, to_apply=%region_4.6 | all-reduce | flops 768 | bytes 6144 | tf_op jit(solution)/shard_map/psum | solution.py:83
  54.6 4.6 %all_gather.6 = bf16[16,2048]{1,0:T(8,128)(2,1)S(1)} all-gather(bf16[16,1024]{1,0:T(8,128)(2,1)S(1)} %fusion.6), channel_id=1, replica_groups=mesh['parts'=2,'sub'=4,'row'=2,'col'=2] {'row'}, dimensions={1}, use_global_device_ids=true | all-gather | bytes 98304 | tf_op jit(solution)/shard_map/all_gather | solution.py:89
  59.2 3.8 %collective-permute-start.3 = (bf16[16,1024]{1,0:T(8,128)(2,1)S(1)}, bf16[16,1024]{1,0:T(8,128)(2,1)S(1)}, u32[]{:S(2)}, u32[]{:S(2)}) collective-permute-start(bf16[16,1024]{1,0:T(8,128)(2,1)S(1)} %get-tuple-element.103), channel_id=1, source_target_pairs={{0,12},{4,0},{8,4},{12,8},{1,13},{5,1},{9,5},{13,9},{2,14},{6,2},{... | collective-permute-start | bytes 98312 | tf_op jit(solution)/shard_map/ppermute | solution.py:13
  63.1 1.9 %collective-permute-done.2 = bf16[16,1024]{1,0:T(8,128)(2,1)S(1)} collective-permute-done((bf16[16,1024]{1,0:T(8,128)(2,1)S(1)}, bf16[16,1024]{1,0:T(8,128)(2,1)S(1)}, u32[]{:S(2)}, u32[]{:S(2)}) %collective-permute-start.2) | collective-permute-done | bytes 32800 | tf_op jit(solution)/shard_map/ppermute | solution.py:13
  65.1 2.8 %gather_fusion.2 = f32[1024,16]{1,0:T(8,128)S(1)} fusion(f32[16,1024]{0,1:T(8,128)S(1)} %copy.23, s32[1024]{0:T(1024)S(1)} %fusion.37), kind=kCustom, calls=%fused_computation.1.clone | custom fusion | bytes 135168 | tf_op jit(solution)/shard_map/jit(_take)/gather | solution.py:96
  68.2 2.8 %gather_fusion.3 = f32[1024,16]{1,0:T(8,128)S(1)} fusion(f32[16,1024]{0,1:T(8,128)S(1)} %copy.25, s32[1024]{0:T(1024)S(1)} %fusion.36), kind=kCustom, calls=%fused_computation.2.clone | custom fusion | bytes 135168 | tf_op jit(solution)/shard_map/jit(_take)/gather | solution.py:97
  71.3 9.1 %all-reduce.1 = (f32[16]{0:T(128)S(1)}, f32[16]{0:T(128)S(1)}) all-reduce(f32[16]{0:T(128)S(1)} %get-tuple-element.64, f32[16]{0:T(128)S(1)} %get-tuple-element.63), channel_id=1, replica_groups=mesh['parts'=2,'sub'=4,'row'=2,'col'=2] {'sub'}, use_global_device_ids=true, to_apply=%region_1.3 | all-reduce | flops 32 | bytes 256 | tf_op jit(solution)/shard_map/psum | solution.py:21
  80.6 10.3 %while.21 = (s32[]{:T(128)}, f32[16,1024]{1,0:T(8,128)S(1)}, s32[]{:T(128)}, bf16[1024,2048]{1,0:T(8,128)(2,1)}, bf16[16,2048]{1,0:T(8,128)(2,1)S(1)}, /*index=5*/s32[]{:T(128)}, s32[]{:T(128)}, s32[]{:T(128)}, s32[]{:T(128)}) while((s32[]{:T(128)}, f32[16,1024]{1,0:T(8,128)S(1)}, s32[]{:T(128)}, bf16[1024,2048]{1,0:T(8,128)(2,1)}, ...), condition=%wide.region_10.12_spmd, body=%wide.region_9.11_spmd.sunk | while | flops 8388614 | bytes 599179 | solution.py:33
  81.9 1.3 fusion.75
  84.5 1.3 fusion.75
  85.8 1.3 fusion.75
  87.1 1.3 fusion.75
  91.2 18.7 %psum.46 = f32[16,48]{1,0:T(8,128)S(1)} all-reduce(f32[16,48]{1,0:T(8,128)S(1)} %fusion.29), channel_id=1, replica_groups=mesh['parts'=2,'sub'=4,'row'=2,'col'=2] {'sub','row'}, use_global_device_ids=true, to_apply=%region_11.13 | all-reduce | flops 768 | bytes 6144 | tf_op jit(solution)/shard_map/psum | solution.py:83
  110.3 4.6 %all_gather.7 = bf16[16,2048]{1,0:T(8,128)(2,1)S(1)} all-gather(bf16[16,1024]{1,0:T(8,128)(2,1)S(1)} %fusion.7), channel_id=1, replica_groups=mesh['parts'=2,'sub'=4,'row'=2,'col'=2] {'row'}, dimensions={1}, use_global_device_ids=true | all-gather | bytes 98304 | tf_op jit(solution)/shard_map/all_gather | solution.py:89
  114.9 2.0 %collective-permute-start.4 = (bf16[16,1024]{1,0:T(8,128)(2,1)S(1)}, bf16[16,1024]{1,0:T(8,128)(2,1)S(1)}, u32[]{:S(2)}, u32[]{:S(2)}) collective-permute-start(bf16[16,1024]{1,0:T(8,128)(2,1)S(1)} %get-tuple-element.101), channel_id=1, source_target_pairs={{0,4},{4,8},{8,12},{12,0},{1,5},{5,9},{9,13},{13,1},{2,6},{6,10},{... | collective-permute-start | bytes 98312 | tf_op jit(solution)/shard_map/ppermute | solution.py:13
  117.0 1.9 %collective-permute-done.5 = bf16[16,1024]{1,0:T(8,128)(2,1)S(1)} collective-permute-done((bf16[16,1024]{1,0:T(8,128)(2,1)S(1)}, bf16[16,1024]{1,0:T(8,128)(2,1)S(1)}, u32[]{:S(2)}, u32[]{:S(2)}) %collective-permute-start.5) | collective-permute-done | bytes 32800 | tf_op jit(solution)/shard_map/ppermute | solution.py:13
  119.0 2.8 %gather_fusion.5 = f32[1024,16]{1,0:T(8,128)S(1)} fusion(f32[16,1024]{0,1:T(8,128)S(1)} %copy.29, s32[1024]{0:T(1024)S(1)} %fusion.36), kind=kCustom, calls=%fused_computation.4.clone | custom fusion | bytes 135168 | tf_op jit(solution)/shard_map/jit(_take)/gather | solution.py:97
  122.1 2.8 %gather_fusion.4 = f32[1024,16]{1,0:T(8,128)S(1)} fusion(f32[16,1024]{0,1:T(8,128)S(1)} %copy.27, s32[1024]{0:T(1024)S(1)} %fusion.37), kind=kCustom, calls=%fused_computation.3.clone | custom fusion | bytes 135168 | tf_op jit(solution)/shard_map/jit(_take)/gather | solution.py:96
  125.3 10.2 %all-reduce = (f32[16]{0:T(128)S(1)}, f32[16]{0:T(128)S(1)}) all-reduce(f32[16]{0:T(128)S(1)} %get-tuple-element.62, f32[16]{0:T(128)S(1)} %get-tuple-element.61), channel_id=1, replica_groups=mesh['parts'=2,'sub'=4,'row'=2,'col'=2] {'sub'}, use_global_device_ids=true, to_apply=%region_8.10 | all-reduce | flops 32 | bytes 256 | tf_op jit(solution)/shard_map/psum | solution.py:21
  (71 shorter events, 17.8 us)
Async XLA Ops:
  0.6 34.3 %copy-start = (bf16[1,24,1024]{2,1,0:T(8,128)(2,1)S(1)}, bf16[1,24,1024]{2,1,0:T(8,128)(2,1)}, u32[]{:S(2)}) copy-start(bf16[1,24,1024]{2,1,0:T(8,128)(2,1)} %param.18) | copy-start | bytes 147460
  0.6 20.7 %copy-start.5 = (f32[1,1024]{1,0:T(1,128)S(1)}, f32[1,1024]{1,0:T(1,128)}, u32[]{:S(2)}) copy-start(f32[1,1024]{1,0:T(1,128)} %param.16) | copy-start | bytes 12292
  0.7 20.6 %copy-start.2 = (s32[1,1024]{1,0:T(1,128)S(1)}, s32[1,1024]{1,0:T(1,128)}, u32[]{:S(2)}) copy-start(s32[1,1024]{1,0:T(1,128)} %param.23) | copy-start | bytes 12292
  1.5 19.8 %collective-permute-start.1 = (bf16[16,1024]{1,0:T(8,128)(2,1)S(1)}, bf16[16,1024]{1,0:T(8,128)(2,1)S(1)}, u32[]{:S(2)}, u32[]{:S(2)}) collective-permute-start(bf16[16,1024]{1,0:T(8,128)(2,1)S(1)} %bitcast_convert_fusion), channel_id=1, source_target_pairs={{0,12},{4,0},{8,4},{12,8},{1,13},{5,1},{9,5},{13,9},{2,14},{6,2},{... | collective-permute-start | bytes 98312 | tf_op jit(solution)/shard_map/ppermute | solution.py:13
  7.3 9.4 %collective-permute-start = (bf16[1,1024]{1,0:T(2,128)(2,1)S(1)}, bf16[1,1024]{1,0:T(2,128)(2,1)S(1)}, u32[]{:S(2)}, u32[]{:S(2)}) collective-permute-start(bf16[1,1024]{1,0:T(2,128)(2,1)S(1)} %convert_element_type.71), channel_id=1, source_target_pairs={{0,12},{4,0},{8,4},{12,8},{1,13},{5,1},{9,5},{13,9},{2,14},{6,2},{... | collective-permute-start | bytes 6152 | tf_op jit(solution)/shard_map/ppermute | solution.py:13
  16.7 37.4 %copy-start.3 = (f32[48,48]{1,0:T(8,128)S(1)}, f32[48,48]{1,0:T(8,128)}, u32[]{:S(2)}) copy-start(f32[48,48]{1,0:T(8,128)} %param.19) | copy-start | bytes 27652
  16.7 46.3 %copy-start.4 = (s32[1,1024]{1,0:T(1,128)S(1)}, s32[1,1024]{1,0:T(1,128)}, u32[]{:S(2)}) copy-start(s32[1,1024]{1,0:T(1,128)} %param.22) | copy-start | bytes 12292
  24.5 46.7 %copy-start.1 = (f32[1,16,1024]{2,1,0:T(8,128)S(1)}, f32[1,16,1024]{2,1,0:T(8,128)}, u32[]{:S(2)}) copy-start(f32[1,16,1024]{2,1,0:T(8,128)} %param.15) | copy-start | bytes 196612
  59.2 5.7 %collective-permute-start.2 = (bf16[16,1024]{1,0:T(8,128)(2,1)S(1)}, bf16[16,1024]{1,0:T(8,128)(2,1)S(1)}, u32[]{:S(2)}, u32[]{:S(2)}) collective-permute-start(bf16[16,1024]{1,0:T(8,128)(2,1)S(1)} %get-tuple-element.102), channel_id=1, source_target_pairs={{0,4},{4,8},{8,12},{12,0},{1,5},{5,9},{9,13},{13,1},{2,6},{6,10},{... | collective-permute-start | bytes 98312 | tf_op jit(solution)/shard_map/ppermute | solution.py:13
  59.2 8.8 %collective-permute-start.3 = (bf16[16,1024]{1,0:T(8,128)(2,1)S(1)}, bf16[16,1024]{1,0:T(8,128)(2,1)S(1)}, u32[]{:S(2)}, u32[]{:S(2)}) collective-permute-start(bf16[16,1024]{1,0:T(8,128)(2,1)S(1)} %get-tuple-element.103), channel_id=1, source_target_pairs={{0,12},{4,0},{8,4},{12,8},{1,13},{5,1},{9,5},{13,9},{2,14},{6,2},{... | collective-permute-start | bytes 98312 | tf_op jit(solution)/shard_map/ppermute | solution.py:13
  114.9 3.9 %collective-permute-start.5 = (bf16[16,1024]{1,0:T(8,128)(2,1)S(1)}, bf16[16,1024]{1,0:T(8,128)(2,1)S(1)}, u32[]{:S(2)}, u32[]{:S(2)}) collective-permute-start(bf16[16,1024]{1,0:T(8,128)(2,1)S(1)} %get-tuple-element.100), channel_id=1, source_target_pairs={{0,12},{4,0},{8,4},{12,8},{1,13},{5,1},{9,5},{13,9},{2,14},{6,2},{... | collective-permute-start | bytes 98312 | tf_op jit(solution)/shard_map/ppermute | solution.py:13
  114.9 7.0 %collective-permute-start.4 = (bf16[16,1024]{1,0:T(8,128)(2,1)S(1)}, bf16[16,1024]{1,0:T(8,128)(2,1)S(1)}, u32[]{:S(2)}, u32[]{:S(2)}) collective-permute-start(bf16[16,1024]{1,0:T(8,128)(2,1)S(1)} %get-tuple-element.101), channel_id=1, source_target_pairs={{0,4},{4,8},{8,12},{12,0},{1,5},{5,9},{9,13},{13,1},{2,6},{6,10},{... | collective-permute-start | bytes 98312 | tf_op jit(solution)/shard_map/ppermute | solution.py:13
where the time goes:
time: 137 us; the launch traced here: 136 us
  blocking collectives  65.9 us (48%)
  matrix products  22.3 us (16%)
  local copies, waits for them, and re-layouts  22.1 us (16%)
  starting transfers between devices  11.4 us (8%)
  other arithmetic  8.41 us (6%)
  waiting for transfers between devices  3.74 us (3%)
  between operations  2.25 us (2%)
    psum x2, blocking collectives, apply_operator(): coarse = lax.psum(scattered, ('sub', 'row'))  37.5 us
    dot_general x16, matrix products, one_tile(): lax.dot_general(vector, piece, (((1,), (1,)), ((), ())), preferred_elemen...  20.7 us
    psum x2, blocking collectives, paired_totals(): lax.psum((inner(residual, precond, half), inner(precond, image, half)), '...  19.2 us
    ppermute x6, starting transfers between devices, shifted(): return lax.ppermute(value, axis, pairs)  11.4 us
    all_gather x2, blocking collectives, apply_operator(): lax.all_gather(united.astype(jnp.bfloat16), 'row', axis=1, tiled=True)  9.15 us
    gather x4, local copies, waits for them, and re-layouts, apply_operator(): jnp.take(arrived_right, right_map, axis=1)  5.95 us
    gather x4, local copies, waits for them, and re-layouts, apply_operator(): result_left = (lower + jnp.take(arrived_left, left_map, axis=1)) * live_left  5.95 us
    gather x1, local copies, waits for them, and re-layouts, per_device(): right_weight = jnp.take(received[1], right_map, axis=1)  4.53 us
  transfers between devices with their start and end apart: 6, of which 2 were waited for; matrix products, arithmetic and copies ran while one was open for 14% of the time, Pallas kernels for 0%

commit v1 on v0

--- a/solution.py
+++ b/solution.py
@@ -80,7 +80,9 @@
             own_slots, coupling, (((1,), (1,)), ((), ())), preferred_element_type=jnp.float32
         )
         scattered = jnp.dot(corner, own_hot, precision=lax.Precision.HIGHEST)
-        coarse = lax.psum(scattered, ("sub", "row"))
+        coarse = scattered
+        for hop_no in ("row", "sub"):
+            coarse = jax.lax.psum(coarse, hop_no)
         solved = jnp.dot(coarse, coarse_inverse, precision=lax.Precision.HIGHEST)
         back = lax.dot_general(
             solved, own_hot, (((1,), (1,)), ((), ())), precision=lax.Precision.HIGHEST

time: 137 us -> 131 us (0.956)
  blocking collectives: 65.9 us -> 59 us
    psum x2 -> x4, blocking collectives: 37.5 us -> 29.9 us  [apply_operator(): coarse = jax.lax.psum(coarse, hop_no)]
  transfers between devices with their start and end apart: 6 -> 6, of which waited for: 2 -> 2; matrix products, arithmetic and copies ran while one was open for 14% -> 15% of each run, Pallas kernels for 0% -> 0%
where the time goes in v1:
time: 131 us; the launch traced here: 129 us
  blocking collectives  59 us (45%)
  matrix products  22.3 us (17%)
  local copies, waits for them, and re-layouts  22.1 us (17%)
  starting transfers between devices  11.4 us (9%)
  other arithmetic  8.41 us (6%)
  waiting for transfers between devices  3.74 us (3%)
  between operations  2.24 us (2%)
    psum x4, blocking collectives, apply_operator(): coarse = jax.lax.psum(coarse, hop_no)  29.9 us
    dot_general x16, matrix products, one_tile(): lax.dot_general(vector, piece, (((1,), (1,)), ((), ())), preferred_elemen...  20.7 us
    psum x2, blocking collectives, paired_totals(): lax.psum((inner(residual, precond, half), inner(precond, image, half)), '...  19.9 us
    ppermute x6, starting transfers between devices, shifted(): return lax.ppermute(value, axis, pairs)  11.4 us
    all_gather x2, blocking collectives, apply_operator(): lax.all_gather(united.astype(jnp.bfloat16), 'row', axis=1, tiled=True)  9.15 us
    gather x4, local copies, waits for them, and re-layouts, apply_operator(): jnp.take(arrived_right, right_map, axis=1)  5.95 us
    gather x4, local copies, waits for them, and re-layouts, apply_operator(): result_left = (lower + jnp.take(arrived_left, left_map, axis=1)) * live_left  5.95 us
    gather x1, local copies, waits for them, and re-layouts, per_device(): right_weight = jnp.take(received[1], right_map, axis=1)  4.53 us
  transfers between devices with their start and end apart: 6, of which 2 were waited for; matrix products, arithmetic and copies ran while one was open for 15% of the time, Pallas kernels for 0%

profile of v1, /device:TPU:0, one launch (start us, length us, event | category | flops | bytes accessed | tf_op | source)
XLA Modules:
  0.0 129.2 jit_solution(6204381350841478852)
XLA Ops:
  1.5 5.1 %collective-permute-start.1 = (bf16[16,1024]{1,0:T(8,128)(2,1)S(1)}, bf16[16,1024]{1,0:T(8,128)(2,1)S(1)}, u32[]{:S(2)}, u32[]{:S(2)}) collective-permute-start(bf16[16,1024]{1,0:T(8,128)(2,1)S(1)} %bitcast_convert_fusion), channel_id=1, source_target_pairs={{0,12},{4,0},{8,4},{12,8},{1,13},{5,1},{9,5},{13,9},{2,14},{6,2},{... | collective-permute-start | bytes 98312 | tf_op jit(solution)/shard_map/ppermute | solution.py:13
  9.1 1.3 %fusion.49 = (s32[1]{0:T(128)}, s32[1]{0:T(128)}) fusion(s32[4]{0:T(128)} %param.21, s32[]{:T(128)S(6)} %select_n.67, s32[]{:T(128)S(6)} %select_n.63), kind=kLoop, calls=%fused_computation.93 | loop fusion | bytes 24 | tf_op jit(solution)/shard_map/dynamic_slice | solution.py:64
  10.5 1.3 %fusion.35 = (f32[1024]{0:T(1024)S(1)}, pred[1024]{0:T(1024)(128)(4,1)S(1)}) fusion(s32[]{:T(128)} %bitcast.3, s32[1024]{0:T(1024)} %bitcast.83), kind=kLoop, calls=%fused_computation.78 | loop fusion | flops 8192 | bytes 9220 | tf_op jit(solution)/shard_map/convert_element_type | solution.py:65
  11.8 1.3 %compare_convert_fusion = f32[1,1024]{1,0:T(1,128)S(1)} fusion(s32[1,1024]{1,0:T(1,128)} %param.23, s32[]{:T(128)} %bitcast.11), kind=kLoop, calls=%fused_computation.65 | loop fusion | flops 2048 | bytes 8196 | tf_op jit(solution)/shard_map/mul | solution.py:106
  16.7 4.5 %gather_fusion = f32[1024]{0:T(1024)S(1)} fusion(f32[1024]{0:T(1024)S(1)} %bitcast.80, s32[1024]{0:T(1024)S(1)} %broadcast_clamp_fusion), kind=kCustom, calls=%fused_computation.5 | custom fusion | bytes 12288 | tf_op jit(solution)/shard_map/jit(_take)/gather | solution.py:107
  21.5 2.8 %gather_fusion.1 = f32[1024,16]{1,0:T(8,128)S(1)} fusion(f32[16,1024]{0,1:T(8,128)S(1)} %copy.21, s32[1024]{0:T(1024)S(1)} %fusion.36), kind=kCustom, calls=%fused_computation.clone | custom fusion | bytes 135168 | tf_op jit(solution)/shard_map/jit(_take)/gather | solution.py:106
  24.5 10.4 %while.20 = (s32[]{:T(128)}, f32[16,1024]{1,0:T(8,128)S(1)}, s32[]{:T(128)}, bf16[1024,2048]{1,0:T(8,128)(2,1)}, bf16[16,2048]{1,0:T(8,128)(2,1)S(1)}, /*index=5*/s32[]{:T(128)}, s32[]{:T(128)}, s32[]{:T(128)}, s32[]{:T(128)}) while((s32[]{:T(128)}, f32[16,1024]{1,0:T(8,128)S(1)}, s32[]{:T(128)}, bf16[1024,2048]{1,0:T(8,128)(2,1)}, ...), condition=%wide.region_3.5_spmd, body=%wide.region_2.4_spmd.sunk | while | flops 8388614 | bytes 599179 | solution.py:33
  25.9 1.3 %fusion.72 = f32[16,1024]{1,0:T(8,128)S(1)} fusion(f32[16,1024]{1,0:T(8,128)S(1)} %get-tuple-element.184, s32[]{:T(128)S(6)} %select_n.118, bf16[16,2048]{1,0:T(8,128)(2,1)S(1)} %get-tuple-element.196, bf16[1024,2048]{1,0:T(8,128)(2,1)} %get-tuple-element.195), kind=kOutput, calls=%fused_computation.7.clone.1 | convolution fusion | flops 8388608 | bytes 599040 | tf_op jit(solution)/shard_map/while/body/dot_general | solution.py:28
  27.1 1.3 %fusion.72 = f32[16,1024]{1,0:T(8,128)S(1)} fusion(f32[16,1024]{1,0:T(8,128)S(1)} %get-tuple-element.184, s32[]{:T(128)S(6)} %select_n.118, bf16[16,2048]{1,0:T(8,128)(2,1)S(1)} %get-tuple-element.196, bf16[1024,2048]{1,0:T(8,128)(2,1)} %get-tuple-element.195), kind=kOutput, calls=%fused_computation.7.clone.1 | convolution fusion | flops 8388608 | bytes 599040 | tf_op jit(solution)/shard_map/while/body/dot_general | solution.py:28
  28.4 1.3 %fusion.72 = f32[16,1024]{1,0:T(8,128)S(1)} fusion(f32[16,1024]{1,0:T(8,128)S(1)} %get-tuple-element.184, s32[]{:T(128)S(6)} %select_n.118, bf16[16,2048]{1,0:T(8,128)(2,1)S(1)} %get-tuple-element.196, bf16[1024,2048]{1,0:T(8,128)(2,1)} %get-tuple-element.195), kind=kOutput, calls=%fused_computation.7.clone.1 | convolution fusion | flops 8388608 | bytes 599040 | tf_op jit(solution)/shard_map/while/body/dot_general | solution.py:28
  31.0 1.3 %fusion.72 = f32[16,1024]{1,0:T(8,128)S(1)} fusion(f32[16,1024]{1,0:T(8,128)S(1)} %get-tuple-element.184, s32[]{:T(128)S(6)} %select_n.118, bf16[16,2048]{1,0:T(8,128)(2,1)S(1)} %get-tuple-element.196, bf16[1024,2048]{1,0:T(8,128)(2,1)} %get-tuple-element.195), kind=kOutput, calls=%fused_computation.7.clone.1 | convolution fusion | flops 8388608 | bytes 599040 | tf_op jit(solution)/shard_map/while/body/dot_general | solution.py:28
  32.3 1.3 %fusion.72 = f32[16,1024]{1,0:T(8,128)S(1)} fusion(f32[16,1024]{1,0:T(8,128)S(1)} %get-tuple-element.184, s32[]{:T(128)S(6)} %select_n.118, bf16[16,2048]{1,0:T(8,128)(2,1)S(1)} %get-tuple-element.196, bf16[1024,2048]{1,0:T(8,128)(2,1)} %get-tuple-element.195), kind=kOutput, calls=%fused_computation.7.clone.1 | convolution fusion | flops 8388608 | bytes 599040 | tf_op jit(solution)/shard_map/while/body/dot_general | solution.py:28
  33.6 1.3 %fusion.72 = f32[16,1024]{1,0:T(8,128)S(1)} fusion(f32[16,1024]{1,0:T(8,128)S(1)} %get-tuple-element.184, s32[]{:T(128)S(6)} %select_n.118, bf16[16,2048]{1,0:T(8,128)(2,1)S(1)} %get-tuple-element.196, bf16[1024,2048]{1,0:T(8,128)(2,1)} %get-tuple-element.195), kind=kOutput, calls=%fused_computation.7.clone.1 | convolution fusion | flops 8388608 | bytes 599040 | tf_op jit(solution)/shard_map/while/body/dot_general | solution.py:28
  35.3 5.0 %psum.57 = f32[16,48]{1,0:T(8,128)S(1)} all-reduce(f32[16,48]{1,0:T(8,128)S(1)} %fusion.30), channel_id=1, replica_groups=mesh['parts'=2,'sub'=4,'row'=2,'col'=2] {'row'}, use_global_device_ids=true, to_apply=%region_4.6 | all-reduce | flops 768 | bytes 6144 | tf_op jit(solution)/shard_map/psum | solution.py:85
  40.2 10.1 %psum.58 = f32[16,48]{1,0:T(8,128)S(1)} all-reduce(f32[16,48]{1,0:T(8,128)S(1)} %psum.57), channel_id=1, replica_groups=mesh['parts'=2,'sub'=4,'row'=2,'col'=2] {'sub'}, use_global_device_ids=true, to_apply=%region_5.7 | all-reduce | flops 768 | bytes 6144 | tf_op jit(solution)/shard_map/psum | solution.py:85
  50.9 4.6 %all_gather.6 = bf16[16,2048]{1,0:T(8,128)(2,1)S(1)} all-gather(bf16[16,1024]{1,0:T(8,128)(2,1)S(1)} %fusion.6), channel_id=1, replica_groups=mesh['parts'=2,'sub'=4,'row'=2,'col'=2] {'row'}, dimensions={1}, use_global_device_ids=true | all-gather | bytes 98304 | tf_op jit(solution)/shard_map/all_gather | solution.py:91
  55.8 3.5 %collective-permute-start.3 = (bf16[16,1024]{1,0:T(8,128)(2,1)S(1)}, bf16[16,1024]{1,0:T(8,128)(2,1)S(1)}, u32[]{:S(2)}, u32[]{:S(2)}) collective-permute-start(bf16[16,1024]{1,0:T(8,128)(2,1)S(1)} %get-tuple-element.103), channel_id=1, source_target_pairs={{0,12},{4,0},{8,4},{12,8},{1,13},{5,1},{9,5},{13,9},{2,14},{6,2},{... | collective-permute-start | bytes 98312 | tf_op jit(solution)/shard_map/ppermute | solution.py:13
  59.3 1.9 %collective-permute-done.2 = bf16[16,1024]{1,0:T(8,128)(2,1)S(1)} collective-permute-done((bf16[16,1024]{1,0:T(8,128)(2,1)S(1)}, bf16[16,1024]{1,0:T(8,128)(2,1)S(1)}, u32[]{:S(2)}, u32[]{:S(2)}) %collective-permute-start.2) | collective-permute-done | bytes 32800 | tf_op jit(solution)/shard_map/ppermute | solution.py:13
  61.3 2.8 %gather_fusion.2 = f32[1024,16]{1,0:T(8,128)S(1)} fusion(f32[16,1024]{0,1:T(8,128)S(1)} %copy.23, s32[1024]{0:T(1024)S(1)} %fusion.37), kind=kCustom, calls=%fused_computation.1.clone | custom fusion | bytes 135168 | tf_op jit(solution)/shard_map/jit(_take)/gather | solution.py:98
  64.4 2.8 %gather_fusion.3 = f32[1024,16]{1,0:T(8,128)S(1)} fusion(f32[16,1024]{0,1:T(8,128)S(1)} %copy.25, s32[1024]{0:T(1024)S(1)} %fusion.36), kind=kCustom, calls=%fused_computation.2.clone | custom fusion | bytes 135168 | tf_op jit(solution)/shard_map/jit(_take)/gather | solution.py:99
  67.6 9.1 %all-reduce.1 = (f32[16]{0:T(128)S(1)}, f32[16]{0:T(128)S(1)}) all-reduce(f32[16]{0:T(128)S(1)} %get-tuple-element.64, f32[16]{0:T(128)S(1)} %get-tuple-element.63), channel_id=1, replica_groups=mesh['parts'=2,'sub'=4,'row'=2,'col'=2] {'sub'}, use_global_device_ids=true, to_apply=%region_1.3 | all-reduce | flops 32 | bytes 256 | tf_op jit(solution)/shard_map/psum | solution.py:21
  76.9 10.3 %while.21 = (s32[]{:T(128)}, f32[16,1024]{1,0:T(8,128)S(1)}, s32[]{:T(128)}, bf16[1024,2048]{1,0:T(8,128)(2,1)}, bf16[16,2048]{1,0:T(8,128)(2,1)S(1)}, /*index=5*/s32[]{:T(128)}, s32[]{:T(128)}, s32[]{:T(128)}, s32[]{:T(128)}) while((s32[]{:T(128)}, f32[16,1024]{1,0:T(8,128)S(1)}, s32[]{:T(128)}, bf16[1024,2048]{1,0:T(8,128)(2,1)}, ...), condition=%wide.region_11.13_spmd, body=%wide.region_10.12_spmd.sunk | while | flops 8388614 | bytes 599179 | solution.py:33
  79.4 1.3 %fusion.75 = f32[16,1024]{1,0:T(8,128)S(1)} fusion(f32[16,1024]{1,0:T(8,128)S(1)} %get-tuple-element.211, s32[]{:T(128)S(6)} %select_n.119, bf16[16,2048]{1,0:T(8,128)(2,1)S(1)} %get-tuple-element.223, bf16[1024,2048]{1,0:T(8,128)(2,1)} %get-tuple-element.222), kind=kOutput, calls=%fused_computation.11.clone.1 | convolution fusion | flops 8388608 | bytes 599040 | tf_op jit(solution)/shard_map/while/body/dot_general | solution.py:28
  80.7 1.3 %fusion.75 = f32[16,1024]{1,0:T(8,128)S(1)} fusion(f32[16,1024]{1,0:T(8,128)S(1)} %get-tuple-element.211, s32[]{:T(128)S(6)} %select_n.119, bf16[16,2048]{1,0:T(8,128)(2,1)S(1)} %get-tuple-element.223, bf16[1024,2048]{1,0:T(8,128)(2,1)} %get-tuple-element.222), kind=kOutput, calls=%fused_computation.11.clone.1 | convolution fusion | flops 8388608 | bytes 599040 | tf_op jit(solution)/shard_map/while/body/dot_general | solution.py:28
  87.4 5.0 %psum.61 = f32[16,48]{1,0:T(8,128)S(1)} all-reduce(f32[16,48]{1,0:T(8,128)S(1)} %fusion.29), channel_id=1, replica_groups=mesh['parts'=2,'sub'=4,'row'=2,'col'=2] {'row'}, use_global_device_ids=true, to_apply=%region_12.14 | all-reduce | flops 768 | bytes 6144 | tf_op jit(solution)/shard_map/psum | solution.py:85
  92.4 9.8 %psum.62 = f32[16,48]{1,0:T(8,128)S(1)} all-reduce(f32[16,48]{1,0:T(8,128)S(1)} %psum.61), channel_id=1, replica_groups=mesh['parts'=2,'sub'=4,'row'=2,'col'=2] {'sub'}, use_global_device_ids=true, to_apply=%region_13.15 | all-reduce | flops 768 | bytes 6144 | tf_op jit(solution)/shard_map/psum | solution.py:85
  102.7 4.6 %all_gather.7 = bf16[16,2048]{1,0:T(8,128)(2,1)S(1)} all-gather(bf16[16,1024]{1,0:T(8,128)(2,1)S(1)} %fusion.7), channel_id=1, replica_groups=mesh['parts'=2,'sub'=4,'row'=2,'col'=2] {'row'}, dimensions={1}, use_global_device_ids=true | all-gather | bytes 98304 | tf_op jit(solution)/shard_map/all_gather | solution.py:91
  108.0 1.3 %collective-permute-start.4 = (bf16[16,1024]{1,0:T(8,128)(2,1)S(1)}, bf16[16,1024]{1,0:T(8,128)(2,1)S(1)}, u32[]{:S(2)}, u32[]{:S(2)}) collective-permute-start(bf16[16,1024]{1,0:T(8,128)(2,1)S(1)} %get-tuple-element.101), channel_id=1, source_target_pairs={{0,4},{4,8},{8,12},{12,0},{1,5},{5,9},{9,13},{13,1},{2,6},{6,10},{... | collective-permute-start | bytes 98312 | tf_op jit(solution)/shard_map/ppermute | solution.py:13
  109.3 1.9 %collective-permute-done.5 = bf16[16,1024]{1,0:T(8,128)(2,1)S(1)} collective-permute-done((bf16[16,1024]{1,0:T(8,128)(2,1)S(1)}, bf16[16,1024]{1,0:T(8,128)(2,1)S(1)}, u32[]{:S(2)}, u32[]{:S(2)}) %collective-permute-start.5) | collective-permute-done | bytes 32800 | tf_op jit(solution)/shard_map/ppermute | solution.py:13
  111.3 2.8 %gather_fusion.5 = f32[1024,16]{1,0:T(8,128)S(1)} fusion(f32[16,1024]{0,1:T(8,128)S(1)} %copy.29, s32[1024]{0:T(1024)S(1)} %fusion.36), kind=kCustom, calls=%fused_computation.4.clone | custom fusion | bytes 135168 | tf_op jit(solution)/shard_map/jit(_take)/gather | solution.py:99
  114.5 2.8 %gather_fusion.4 = f32[1024,16]{1,0:T(8,128)S(1)} fusion(f32[16,1024]{0,1:T(8,128)S(1)} %copy.27, s32[1024]{0:T(1024)S(1)} %fusion.37), kind=kCustom, calls=%fused_computation.3.clone | custom fusion | bytes 135168 | tf_op jit(solution)/shard_map/jit(_take)/gather | solution.py:98
  117.6 10.9 %all-reduce = (f32[16]{0:T(128)S(1)}, f32[16]{0:T(128)S(1)}) all-reduce(f32[16]{0:T(128)S(1)} %get-tuple-element.62, f32[16]{0:T(128)S(1)} %get-tuple-element.61), channel_id=1, replica_groups=mesh['parts'=2,'sub'=4,'row'=2,'col'=2] {'sub'}, use_global_device_ids=true, to_apply=%region_9.11 | all-reduce | flops 32 | bytes 256 | tf_op jit(solution)/shard_map/psum | solution.py:21
  (73 shorter events, 21.4 us)
Async XLA Ops:
  0.6 34.3 %copy-start = (bf16[1,24,1024]{2,1,0:T(8,128)(2,1)S(1)}, bf16[1,24,1024]{2,1,0:T(8,128)(2,1)}, u32[]{:S(2)}) copy-start(bf16[1,24,1024]{2,1,0:T(8,128)(2,1)} %param.18) | copy-start | bytes 147460
  0.6 20.7 %copy-start.5 = (f32[1,1024]{1,0:T(1,128)S(1)}, f32[1,1024]{1,0:T(1,128)}, u32[]{:S(2)}) copy-start(f32[1,1024]{1,0:T(1,128)} %param.16) | copy-start | bytes 12292
  0.7 20.6 %copy-start.2 = (s32[1,1024]{1,0:T(1,128)S(1)}, s32[1,1024]{1,0:T(1,128)}, u32[]{:S(2)}) copy-start(s32[1,1024]{1,0:T(1,128)} %param.23) | copy-start | bytes 12292
  1.5 19.8 %collective-permute-start.1 = (bf16[16,1024]{1,0:T(8,128)(2,1)S(1)}, bf16[16,1024]{1,0:T(8,128)(2,1)S(1)}, u32[]{:S(2)}, u32[]{:S(2)}) collective-permute-start(bf16[16,1024]{1,0:T(8,128)(2,1)S(1)} %bitcast_convert_fusion), channel_id=1, source_target_pairs={{0,12},{4,0},{8,4},{12,8},{1,13},{5,1},{9,5},{13,9},{2,14},{6,2},{... | collective-permute-start | bytes 98312 | tf_op jit(solution)/shard_map/ppermute | solution.py:13
  7.3 9.4 %collective-permute-start = (bf16[1,1024]{1,0:T(2,128)(2,1)S(1)}, bf16[1,1024]{1,0:T(2,128)(2,1)S(1)}, u32[]{:S(2)}, u32[]{:S(2)}) collective-permute-start(bf16[1,1024]{1,0:T(2,128)(2,1)S(1)} %convert_element_type.71), channel_id=1, source_target_pairs={{0,12},{4,0},{8,4},{12,8},{1,13},{5,1},{9,5},{13,9},{2,14},{6,2},{... | collective-permute-start | bytes 6152 | tf_op jit(solution)/shard_map/ppermute | solution.py:13
  16.7 33.6 %copy-start.3 = (f32[48,48]{1,0:T(8,128)S(1)}, f32[48,48]{1,0:T(8,128)}, u32[]{:S(2)}) copy-start(f32[48,48]{1,0:T(8,128)} %param.19) | copy-start | bytes 27652
  16.7 42.5 %copy-start.4 = (s32[1,1024]{1,0:T(1,128)S(1)}, s32[1,1024]{1,0:T(1,128)}, u32[]{:S(2)}) copy-start(s32[1,1024]{1,0:T(1,128)} %param.22) | copy-start | bytes 12292
  24.5 42.9 %copy-start.1 = (f32[1,16,1024]{2,1,0:T(8,128)S(1)}, f32[1,16,1024]{2,1,0:T(8,128)}, u32[]{:S(2)}) copy-start(f32[1,16,1024]{2,1,0:T(8,128)} %param.15) | copy-start | bytes 196612
  55.4 5.7 %collective-permute-start.2 = (bf16[16,1024]{1,0:T(8,128)(2,1)S(1)}, bf16[16,1024]{1,0:T(8,128)(2,1)S(1)}, u32[]{:S(2)}, u32[]{:S(2)}) collective-permute-start(bf16[16,1024]{1,0:T(8,128)(2,1)S(1)} %get-tuple-element.102), channel_id=1, source_target_pairs={{0,4},{4,8},{8,12},{12,0},{1,5},{5,9},{9,13},{13,1},{2,6},{6,10},{... | collective-permute-start | bytes 98312 | tf_op jit(solution)/shard_map/ppermute | solution.py:13
  55.8 8.5 %collective-permute-start.3 = (bf16[16,1024]{1,0:T(8,128)(2,1)S(1)}, bf16[16,1024]{1,0:T(8,128)(2,1)S(1)}, u32[]{:S(2)}, u32[]{:S(2)}) collective-permute-start(bf16[16,1024]{1,0:T(8,128)(2,1)S(1)} %get-tuple-element.103), channel_id=1, source_target_pairs={{0,12},{4,0},{8,4},{12,8},{1,13},{5,1},{9,5},{13,9},{2,14},{6,2},{... | collective-permute-start | bytes 98312 | tf_op jit(solution)/shard_map/ppermute | solution.py:13
  107.3 3.9 %collective-permute-start.5 = (bf16[16,1024]{1,0:T(8,128)(2,1)S(1)}, bf16[16,1024]{1,0:T(8,128)(2,1)S(1)}, u32[]{:S(2)}, u32[]{:S(2)}) collective-permute-start(bf16[16,1024]{1,0:T(8,128)(2,1)S(1)} %get-tuple-element.100), channel_id=1, source_target_pairs={{0,12},{4,0},{8,4},{12,8},{1,13},{5,1},{9,5},{13,9},{2,14},{6,2},{... | collective-permute-start | bytes 98312 | tf_op jit(solution)/shard_map/ppermute | solution.py:13
  108.0 6.3 %collective-permute-start.4 = (bf16[16,1024]{1,0:T(8,128)(2,1)S(1)}, bf16[16,1024]{1,0:T(8,128)(2,1)S(1)}, u32[]{:S(2)}, u32[]{:S(2)}) collective-permute-start(bf16[16,1024]{1,0:T(8,128)(2,1)S(1)} %get-tuple-element.101), channel_id=1, source_target_pairs={{0,4},{4,8},{8,12},{12,0},{1,5},{5,9},{9,13},{13,1},{2,6},{6,10},{... | collective-permute-start | bytes 98312 | tf_op jit(solution)/shard_map/ppermute | solution.py:13
